TPU v7x, 256 devices: a whole 4x4x8 slice. The times are simulated.
256 devices in a mesh: req: 4 (over y), vocab: 64 (over z, x, core).
Axes of the slice: x: 4, y: 4, z: 8, core: 2. Of those that a mesh axis runs over, the one named last changes fastest.
Arguments:
- hidden: bfloat16 [8192, 4096], P('req', 'vocab'), may hold values from -320 to 320
- gain: float32 [4096], replicated, may hold values from 0.5 to 1.5
- head: bfloat16 [4096, 32768], P(None, ('req', 'vocab'))
- targets: int32 [8192], P('req'), may hold values from 0 to 32767
- lengths: int32 [4, 4], P('req'), may hold values from 1 to 1280, 2048 in all within a row
Outputs:
- token_logprob: float32 [8192], P(('req', 'vocab'))
- token_entropy: float32 [8192], P(('req', 'vocab'))
- seq_logprob: float32 [12], P('req')
- seq_entropy: float32 [12], P('req')
Inputs may be any that keep to these rules, and one draw needn't show every extreme that they name: lengths[q, 3] counts the empty slots at the end of index q's rows.
All inputs are finite; a program needn't handle non-finite values.
Results may differ from a plain program's by a relative error of at most 0.0012.
Values may be sent and summed in bfloat16 or wider, within the bound.
A program may use at most 128 MiB of HBM per device.

v0:
```python
import jax
import jax.numpy as jnp
from jax import lax
from jax.sharding import Mesh
from jax.sharding import PartitionSpec as P

D = 4096
SEQ_DEV = 3
VOCAB = ("vocab_0", "vocab_1", "vocab_2")
REQ_VOCAB = ("req", "vocab_0", "vocab_1", "vocab_2")
EPS = 1e-05


def gathered_once(shard, axis):
    leaves = jax.tree.leaves(shard)
    order = sorted(range(len(leaves)), key=lambda k: -leaves[k].size)
    width = (1, *leaves[order[0]].shape)[-1]
    lines = [
        jnp.pad(leaves[k].reshape(-1), (0, -leaves[k].size % width)).reshape(-1, width)
        for k in order
    ]
    both, at, found = (lax.all_gather(jnp.concatenate(lines), axis), 0, {})
    for k, line in zip(order, lines):
        slab = both[:, at : at + len(line)].reshape(len(both), -1)
        found[k] = slab[:, : leaves[k].size].reshape(-1, *leaves[k].shape)
        at += len(line)
    numbers = iter(range(len(leaves)))
    return jax.tree.map(lambda _: found[next(numbers)], shard)


def combined_by_axis(shard, axes, combine):
    for axis in axes:
        pieces = gathered_once(shard, axis)
        shard = jax.tree.map(lambda part: part[0], pieces)
        for k in range(1, lax.axis_size(axis)):
            shard = combine(shard, jax.tree.map(lambda part: part[k], pieces))
    return shard


def combine_stats(first, second):
    peak = jnp.maximum(first[0], second[0])
    scale_first = jnp.exp(first[0] - peak)
    scale_second = jnp.exp(second[0] - peak)
    return (
        peak,
        first[1] * scale_first + second[1] * scale_second,
        first[2] * scale_first + second[2] * scale_second,
        first[3] + second[3],
    )


def finish_rows(peak, total, moment, picked):
    log_total = peak + jnp.log(total)
    return (picked - log_total, log_total - moment / total)


def shards(hidden, gain, head, targets, lengths):
    rows = hidden.shape[0]
    vocab_index = lax.axis_index(VOCAB)
    vocab_count = lax.axis_size(VOCAB)
    shard_cols = head.shape[1]
    width_cols = shard_cols * lax.axis_size("req")
    col_pos = jnp.arange(width_cols, dtype=jnp.int32)
    col_ids = (
        col_pos // shard_cols * (vocab_count * shard_cols)
        + vocab_index * shard_cols
        + col_pos % shard_cols
    )
    block = min(512, rows)
    count = rows // block
    seq_lens = lengths[0, :SEQ_DEV]
    ends = jnp.cumsum(seq_lens)
    starts = ends - seq_lens
    live = ends[-1]
    full_rows = lax.all_gather(hidden, VOCAB, axis=1, tiled=True)
    values = full_rows.astype(jnp.float32)
    mean_sq = jnp.sum(values * values, axis=1) / D
    normed = (values * lax.rsqrt(mean_sq + EPS)[:, None] * gain[None, :]).astype(jnp.bfloat16)
    columns = lax.all_gather(head, "req", axis=1, tiled=True)

    def block_logits(start):
        rows_blk = lax.dynamic_slice_in_dim(normed, start, block, 0)
        return jnp.dot(rows_blk, columns, preferred_element_type=jnp.float32)

    def compute_block(start):
        logits = block_logits(start)
        wanted = lax.dynamic_slice_in_dim(targets, start, block, 0)
        peak = jnp.max(logits, axis=1)
        weights = jnp.exp(logits - peak[:, None])
        total = jnp.sum(weights, axis=1)
        moment = jnp.sum(weights * logits, axis=1)
        picked = jnp.sum(jnp.where(col_ids[None, :] == wanted[:, None], logits, 0.0), axis=1)
        return (peak, total, moment, picked)

    def one_block(block_index):
        start = block_index * block
        return compute_block(start)

    peak, total, moment, picked = lax.map(one_block, jnp.arange(count, dtype=jnp.int32))
    peak = peak.reshape(rows)
    total = total.reshape(rows)
    moment = moment.reshape(rows)
    picked = picked.reshape(rows)
    share = rows // vocab_count
    divisor = seq_lens.astype(jnp.float32)
    peak, total, moment, picked = combined_by_axis(
        (peak, total, moment, picked), VOCAB, combine_stats
    )
    logprob, entropy = finish_rows(peak, total, moment, picked)
    local = jnp.arange(rows, dtype=jnp.int32)
    valid = local < live
    logprob = jnp.where(valid, logprob, 0.0)
    entropy = jnp.where(valid, entropy, 0.0)
    member = ((local[None, :] >= starts[:, None]) & (local[None, :] < ends[:, None])).astype(
        jnp.float32
    )
    seq_lp = jnp.sum(member * logprob[None, :], axis=1) / divisor
    seq_ent = jnp.sum(member * entropy[None, :], axis=1) / divisor
    own_lp = lax.dynamic_slice_in_dim(logprob, vocab_index * share, share, 0)
    own_ent = lax.dynamic_slice_in_dim(entropy, vocab_index * share, share, 0)
    return (own_lp, own_ent, seq_lp, seq_ent)


def solution(mesh):
    split = Mesh(
        mesh.devices.reshape(mesh.shape["req"], 8, 4, 2), ("req", "vocab_0", "vocab_1", "vocab_2")
    )
    placed = (P("req", VOCAB), P(), P(None, REQ_VOCAB), P("req"), P("req", None))
    return jax.shard_map(
        shards,
        mesh=split,
        in_specs=placed,
        out_specs=(P(REQ_VOCAB), P(REQ_VOCAB), P("req"), P("req")),
        check_vma=False,
    )
```

profile of v0, /device:TPU:1, one launch (start us, length us, event | category | flops | bytes accessed | tf_op | source)
XLA Modules:
  0.0 251.6 jit_solution(500161678944132281)
XLA Ops:
  7.2 0.7 all-gather.9.cloned.1.call-update
  8.0 0.7 all-gather.11.cloned.1.call-update
  8.7 0.7 slice_bitcast_fusion.36
  9.4 0.2 broadcast_in_dim.39
  9.5 0.6 slice.300
  10.1 0.7 bitcast_subtract_fusion
  10.8 103.4 %all-gather.9.cloned.1.call-done = bf16[2048,4096]{0,1:T(8,128)(2,1)} async-done(((bf16[2048,64]{0,1:T(8,128)(2,1)}), bf16[2048,4096]{0,1:T(8,128)(2,1)}) %all-gather.9.cloned.1.call-update) | async-done | bytes 16777232 | tf_op jit(solution)/shard_map/all_gather | solution.py:75
  114.2 7.7 %fusion.16 = f32[2048]{0:T(1024)S(1)} fusion(bf16[2048,4096]{0,1:T(8,128)(2,1)} %all-gather.9.cloned.1.call-done), kind=kLoop, calls=%fused_computation.24 | loop fusion | flops 25163776 | bytes 16785408 | tf_op jit(solution)/shard_map/reduce_sum | solution.py:77
  121.9 3.4 %copy-done = bf16[2048,4096]{0,1:T(8,128)(2,1)S(1)} copy-done((bf16[2048,4096]{0,1:T(8,128)(2,1)S(1)}, bf16[2048,4096]{0,1:T(8,128)(2,1)}, u32[]{:S(2)}) %copy-start) | copy-done | bytes 16777240
  125.3 8.7 %fusion.18 = bf16[2048,4096]{0,1:T(8,128)(2,1)} fusion(bf16[2048,4096]{0,1:T(8,128)(2,1)S(1)} %copy-done, f32[4096]{0:T(1024)S(1)} %copy-done.1, f32[2048]{0:T(1024)S(1)} %add_rsqrt_fusion), kind=kLoop, calls=%fused_computation.26 | loop fusion | flops 33554432 | bytes 33579008 | tf_op jit(solution)/shard_map/convert_element_type | solution.py:78
  134.0 31.2 %all-gather.11.cloned.1.call-done = bf16[4096,512]{1,0:T(8,128)(2,1)} async-done(((bf16[4096,128]{1,0:T(8,128)(2,1)}), bf16[4096,512]{1,0:T(8,128)(2,1)}) %all-gather.11.cloned.1.call-update) | async-done | bytes 4194320 | tf_op jit(solution)/shard_map/all_gather | solution.py:79
  165.2 33.8 %while.17 = (s32[]{:T(128)}, f32[4,512]{1,0:T(4,128)S(1)}, f32[4,512]{1,0:T(4,128)S(1)}, f32[4,512]{1,0:T(4,128)S(1)}, f32[4,512]{1,0:T(4,128)S(1)}, /*index=5*/...) while((s32[]{:T(128)}, f32[4,512]{1,0:T(4,128)S(1)}, ...), condition=%wide.region_7.8_spmd.clone, body=%wide.region_2.7_spmd.clone.sunk | while | flops 2149586432 | bytes 10522843 | solution.py:99
  165.2 0.6 dynamic_slice.29
  166.5 5.9 %fusion.105 = (f32[512]{0:T(512)S(1)}, f32[512,512]{0,1:T(8,128)S(1)}) fusion(bf16[4096,512]{1,0:T(8,128)(2,1)} %get-tuple-element.256, bf16[2048,4096]{0,1:T(8,128)(2,1)} %get-tuple-element.255, s32[]{:T(128)S(6)} %select_n.72), kind=kOutput, calls=%fused_computation.187.clone.1 | convolution fusion | flops 2147745280 | bytes 9439236 | tf_op jit(solution)/shard_map/while/body/eval_jaxpr/dot_general | solution.py:83
  172.3 0.8 dynamic_slice.30
  173.1 0.3 multiply_reduce_fusion.2
  173.5 0.1 dynamic_update_slice.24
  173.5 0.1 dynamic_update_slice.22
  173.6 0.1 dynamic_update_slice.21
  173.7 0.6 dynamic_slice.29
  174.9 5.9 %fusion.105 = (f32[512]{0:T(512)S(1)}, f32[512,512]{0,1:T(8,128)S(1)}) fusion(bf16[4096,512]{1,0:T(8,128)(2,1)} %get-tuple-element.256, bf16[2048,4096]{0,1:T(8,128)(2,1)} %get-tuple-element.255, s32[]{:T(128)S(6)} %select_n.72), kind=kOutput, calls=%fused_computation.187.clone.1 | convolution fusion | flops 2147745280 | bytes 9439236 | tf_op jit(solution)/shard_map/while/body/eval_jaxpr/dot_general | solution.py:83
  180.8 0.8 dynamic_slice.30
  181.6 0.3 multiply_reduce_fusion.2
  181.9 0.1 dynamic_update_slice.24
  182.0 0.1 dynamic_update_slice.22
  182.1 0.6 dynamic_slice.29
  183.4 5.9 %fusion.105 = (f32[512]{0:T(512)S(1)}, f32[512,512]{0,1:T(8,128)S(1)}) fusion(bf16[4096,512]{1,0:T(8,128)(2,1)} %get-tuple-element.256, bf16[2048,4096]{0,1:T(8,128)(2,1)} %get-tuple-element.255, s32[]{:T(128)S(6)} %select_n.72), kind=kOutput, calls=%fused_computation.187.clone.1 | convolution fusion | flops 2147745280 | bytes 9439236 | tf_op jit(solution)/shard_map/while/body/eval_jaxpr/dot_general | solution.py:83
  189.2 0.8 dynamic_slice.30
  190.0 0.3 multiply_reduce_fusion.2
  190.4 0.1 dynamic_update_slice.24
  190.6 0.6 dynamic_slice.29
  191.8 5.9 %fusion.105 = (f32[512]{0:T(512)S(1)}, f32[512,512]{0,1:T(8,128)S(1)}) fusion(bf16[4096,512]{1,0:T(8,128)(2,1)} %get-tuple-element.256, bf16[2048,4096]{0,1:T(8,128)(2,1)} %get-tuple-element.255, s32[]{:T(128)S(6)} %select_n.72), kind=kOutput, calls=%fused_computation.187.clone.1 | convolution fusion | flops 2147745280 | bytes 9439236 | tf_op jit(solution)/shard_map/while/body/eval_jaxpr/dot_general | solution.py:83
  197.7 0.8 dynamic_slice.30
  198.5 0.3 multiply_reduce_fusion.2
  198.9 0.1 dynamic_update_slice.24
  199.1 20.3 %all-gather.3 = f32[8,4,2048]{2,1,0:T(4,128)S(1)} all-gather(f32[1,4,2048]{2,1,0:T(4,128)S(1)} %maximum_bitcast_fusion), channel_id=2, replica_groups=mesh['req'=4,'vocab_0'=8,'vocab_1'=4,'vocab_2'=2] {'vocab_0'}, dimensions={0}, use_global_device_ids=true | all-gather | bytes 294912 | tf_op jit(solution)/shard_map/all_gather | solution.py:22
  219.4 0.2 fusion.62
  219.6 0.1 fusion.39
  219.7 0.2 fusion.41
  219.9 9.4 %all-gather.4 = f32[4,4,2048]{2,1,0:T(4,128)S(1)} all-gather(f32[1,4,2048]{2,1,0:T(4,128)S(1)} %maximum_bitcast_fusion.1), channel_id=3, replica_groups=mesh['req'=4,'vocab_0'=8,'vocab_1'=4,'vocab_2'=2] {'vocab_1'}, dimensions={0}, use_global_device_ids=true | all-gather | bytes 163840 | tf_op jit(solution)/shard_map/all_gather | solution.py:22
  229.3 0.1 fusion.31
  229.5 0.1 fusion.22
  229.6 12.5 %all-gather.5 = f32[2,4,2048]{2,1,0:T(4,128)S(1)} all-gather(f32[1,4,2048]{2,1,0:T(4,128)S(1)} %maximum_bitcast_fusion.2), channel_id=4, replica_groups=mesh['req'=4,'vocab_0'=8,'vocab_1'=4,'vocab_2'=2] {'vocab_2'}, dimensions={0}, use_global_device_ids=true | all-gather | bytes 98304 | tf_op jit(solution)/shard_map/all_gather | solution.py:22
  242.1 0.7 subtract_select_fusion
  242.8 0.6 dynamic_slice.17
  243.4 0.6 dynamic_slice.16
  244.0 0.2 select_reduce_fusion.1
  244.2 0.5 fusion.92
  (35 shorter events, 0.8 us)
Async XLA Ops:
  7.2 114.7 %copy-start.1 = (f32[4096]{0:T(1024)S(1)}, f32[4096]{0:T(1024)}, u32[]{:S(2)}) copy-start(f32[4096]{0:T(1024)} %param.8) | copy-start | bytes 49156
  7.2 107.0 %all-gather.9.cloned.1.call-start = ((), (), s32[]{:S(2)}) async-start(), calls=%async_computation | async-start | bytes 17039360 | tf_op jit(solution)/shard_map/all_gather | solution.py:75
  7.9 157.3 %all-gather.11.cloned.1.call-start = ((), (), s32[]{:S(2)}) async-start(), calls=%async_computation.1 | async-start | bytes 5242880 | tf_op jit(solution)/shard_map/all_gather | solution.py:79
  114.2 11.1 %copy-start = (bf16[2048,4096]{0,1:T(8,128)(2,1)S(1)}, bf16[2048,4096]{0,1:T(8,128)(2,1)}, u32[]{:S(2)}) copy-start(bf16[2048,4096]{0,1:T(8,128)(2,1)} %all-gather.9.cloned.1.call-done) | copy-start | bytes 50331652
  165.2 79.0 %copy-start.2 = (s32[1,4]{1,0:T(1,128)S(1)}, s32[1,4]{1,0:T(1,128)}, u32[]{:S(2)}) copy-start(s32[1,4]{1,0:T(1,128)} %param.11) | copy-start | bytes 52
Sparse Core Ops, SparseCore 0:
  10.8 103.3 all-gather.8
  116.0 49.1 all-gather.10
where the time goes:
time: 252 us
  waiting for transfers between devices  136 us (54%)
  blocking collectives  42.2 us (17%)
  matrix products  23.5 us (9%)
  other arithmetic  20.9 us (8%)
  between operations  14.2 us (6%)
  local copies, waits for them, and re-layouts  12.1 us (5%)
  loops' own time  2.75 us (1%)
    all_gather x1, waiting for transfers between devices, shards(): full_rows = lax.all_gather(hidden, VOCAB, axis=1, tiled=True)  103 us
    all_gather x3, blocking collectives, gathered_once(): both, at, found = (lax.all_gather(jnp.concatenate(lines), axis), 0, {})  42.2 us
    all_gather x1, waiting for transfers between devices, shards(): columns = lax.all_gather(head, 'req', axis=1, tiled=True)  31.2 us
    dot_general x4, matrix products, block_logits(): return jnp.dot(rows_blk, columns, preferred_element_type=jnp.float32)  23.5 us
    convert_element_type x1, other arithmetic, shards(): (values * lax.rsqrt(mean_sq + EPS)[:, None] * gain[None, :]).astype(jnp.b...  8.73 us
    reduce_sum x1, other arithmetic, shards(): mean_sq = jnp.sum(values * values, axis=1) / D  7.68 us
  transfers between devices with their start and end apart: 2, of which 2 were waited for; matrix products, arithmetic and copies ran while one was open for 7% of the time, Pallas kernels for 0%

commit v1 on v0

--- a/solution.py
+++ b/solution.py
@@ -76,7 +76,9 @@
     values = full_rows.astype(jnp.float32)
     mean_sq = jnp.sum(values * values, axis=1) / D
     normed = (values * lax.rsqrt(mean_sq + EPS)[:, None] * gain[None, :]).astype(jnp.bfloat16)
-    columns = lax.all_gather(head, "req", axis=1, tiled=True)
+    columns = jnp.concatenate(
+        lax.all_to_all(jnp.stack([head] * lax.axis_size("req")), "req", 0, 0), axis=1
+    )
 
     def block_logits(start):
         rows_blk = lax.dynamic_slice_in_dim(normed, start, block, 0)

time: 252 us -> 217 us (0.86)
  waiting for transfers between devices: 136 us -> 83.1 us
  local copies, waits for them, and re-layouts: 12.1 us -> 28.6 us
  starting transfers between devices: 0.08 us -> 5.04 us
  blocking collectives: 42.2 us -> 38.6 us
    all_gather x1, waiting for transfers between devices: 103 us -> 37.3 us  [shards(): full_rows = lax.all_gather(hidden, VOCAB, axis=1, tiled=True)]
    all_to_all x0 -> x1, waiting for transfers between devices: none -> 45.1 us  [shards(): lax.all_to_all(jnp.stack([head] * lax.axis_size('req')), 'req', 0, 0)]
    all_gather x1 -> x0, waiting for transfers between devices: 31.2 us -> none  [shards(): columns = lax.all_gather(head, 'req', axis=1, tiled=True)]
    all_to_all x0 -> x1, local copies, waits for them, and re-layouts: none -> 6.46 us  [shards(): lax.all_to_all(jnp.stack([head] * lax.axis_size('req')), 'req', 0, 0)]
    unnamed x10 -> x11, local copies, waits for them, and re-layouts: 3.44 us -> 9.75 us
    all_to_all x0 -> x1, starting transfers between devices: none -> 5 us  [shards(): lax.all_to_all(jnp.stack([head] * lax.axis_size('req')), 'req', 0, 0)]
    another operation x0 -> x1, local copies, waits for them, and re-layouts: none -> 3.73 us  [shards(): jnp.stack([head] * lax.axis_size('req'))]
    all_gather x3, blocking collectives: 42.2 us -> 38.6 us  [gathered_once(): both, at, found = (lax.all_gather(jnp.concatenate(lines), axis), 0, {})]
  transfers between devices with their start and end apart: 2 -> 2, of which waited for: 2 -> 2; matrix products, arithmetic and copies ran while one was open for 7% -> 9% of each run, Pallas kernels for 0% -> 0%
where the time goes in v1:
time: 217 us; the launch traced here: 216 us
  waiting for transfers between devices  83.1 us (38%)
  blocking collectives  38.6 us (18%)
  local copies, waits for them, and re-layouts  28.6 us (13%)
  matrix products  23.5 us (11%)
  other arithmetic  20.9 us (10%)
  between operations  14.2 us (7%)
  starting transfers between devices  5.04 us (2%)
  loops' own time  2.75 us (1%)
    all_to_all x1, waiting for transfers between devices, shards(): lax.all_to_all(jnp.stack([head] * lax.axis_size('req')), 'req', 0, 0)  45.1 us
    all_gather x3, blocking collectives, gathered_once(): both, at, found = (lax.all_gather(jnp.concatenate(lines), axis), 0, {})  38.6 us
    all_gather x1, waiting for transfers between devices, shards(): full_rows = lax.all_gather(hidden, VOCAB, axis=1, tiled=True)  37.3 us
    dot_general x4, matrix products, block_logits(): return jnp.dot(rows_blk, columns, preferred_element_type=jnp.float32)  23.5 us
    unnamed x11, local copies, waits for them, and re-layouts  9.75 us
    convert_element_type x1, other arithmetic, shards(): (values * lax.rsqrt(mean_sq + EPS)[:, None] * gain[None, :]).astype(jnp.b...  8.73 us
    reduce_sum x1, other arithmetic, shards(): mean_sq = jnp.sum(values * values, axis=1) / D  7.68 us
    all_to_all x1, local copies, waits for them, and re-layouts, shards(): lax.all_to_all(jnp.stack([head] * lax.axis_size('req')), 'req', 0, 0)  6.46 us
  transfers between devices with their start and end apart: 2, of which 2 were waited for; matrix products, arithmetic and copies ran while one was open for 9% of the time, Pallas kernels for 0%

profile of v1, /device:TPU:1, one launch (start us, length us, event | category | flops | bytes accessed | tf_op | source)
XLA Modules:
  0.0 216.5 jit_solution(2645708235544174236)
XLA Ops:
  7.2 0.7 all-gather.8.cloned.1.call-update
  7.9 3.7 %stack.2 = bf16[4,4096,128]{2,1,0:T(8,128)(2,1)} broadcast(bf16[4096,128]{1,0:T(8,128)(2,1)} %param.9), dimensions={1,2} | broadcast | bytes 5242880 | tf_op jit(solution)/shard_map/stack | solution.py:80
  11.6 5.0 %all-to-all-start = ((bf16[4,4096,128]{2,1,0:T(8,128)(2,1)}), bf16[4,4096,128]{2,1,0:T(8,128)(2,1)}, u32[]{:S(2)}, u32[]{:S(2)}) async-start(bf16[4,4096,128]{2,1,0:T(8,128)(2,1)} %stack.2), calls=%async_computation | async-start | bytes 8388608 | tf_op jit(solution)/shard_map/all_to_all | solution.py:80
  16.6 0.7 slice_bitcast_fusion.36
  17.3 0.2 broadcast_in_dim.39
  17.5 0.6 slice.300
  18.1 0.7 bitcast_subtract_fusion
  18.7 45.1 %all-to-all-done = bf16[4,4096,128]{2,1,0:T(8,128)(2,1)} async-done(((bf16[4,4096,128]{2,1,0:T(8,128)(2,1)}), bf16[4,4096,128]{2,1,0:T(8,128)(2,1)}, u32[]{:S(2)}, u32[]{:S(2)}) %all-to-all-start) | async-done | bytes 4194336 | tf_op jit(solution)/shard_map/all_to_all | solution.py:80
  63.8 6.5 %copy.14 = bf16[4,4096,128]{1,2,0:T(8,128)(2,1)} copy(bf16[4,4096,128]{2,1,0:T(8,128)(2,1)} %all-to-all-done) | data formatting | bytes 8388608 | tf_op jit(solution)/shard_map/all_to_all | solution.py:80
  70.2 6.6 %copy.16 = bf16[4096,512]{1,0:T(8,128)(2,1)} copy(bf16[4096,512]{0,1:T(8,128)(2,1)} %bitcast.450) | data formatting | bytes 8388608
  76.9 37.3 %all-gather.8.cloned.1.call-done = bf16[2048,4096]{0,1:T(8,128)(2,1)} async-done(((bf16[2048,64]{0,1:T(8,128)(2,1)}), bf16[2048,4096]{0,1:T(8,128)(2,1)}) %all-gather.8.cloned.1.call-update) | async-done | bytes 16777232 | tf_op jit(solution)/shard_map/all_gather | solution.py:75
  114.2 7.7 %fusion.16 = f32[2048]{0:T(1024)S(1)} fusion(bf16[2048,4096]{0,1:T(8,128)(2,1)} %all-gather.8.cloned.1.call-done), kind=kLoop, calls=%fused_computation.24 | loop fusion | flops 25163776 | bytes 16785408 | tf_op jit(solution)/shard_map/reduce_sum | solution.py:77
  121.9 3.1 %copy-done = bf16[2048,4096]{0,1:T(8,128)(2,1)S(1)} copy-done((bf16[2048,4096]{0,1:T(8,128)(2,1)S(1)}, bf16[2048,4096]{0,1:T(8,128)(2,1)}, u32[]{:S(2)}) %copy-start) | copy-done | bytes 16777240
  125.0 8.7 %fusion.18 = bf16[2048,4096]{0,1:T(8,128)(2,1)} fusion(bf16[2048,4096]{0,1:T(8,128)(2,1)S(1)} %copy-done, f32[4096]{0:T(1024)S(1)} %copy-done.1, f32[2048]{0:T(1024)S(1)} %add_rsqrt_fusion), kind=kLoop, calls=%fused_computation.26 | loop fusion | flops 33554432 | bytes 33579008 | tf_op jit(solution)/shard_map/convert_element_type | solution.py:78
  133.7 33.8 %while.17 = (s32[]{:T(128)}, f32[4,512]{1,0:T(4,128)S(1)}, f32[4,512]{1,0:T(4,128)S(1)}, f32[4,512]{1,0:T(4,128)S(1)}, f32[4,512]{1,0:T(4,128)S(1)}, /*index=5*/...) while((s32[]{:T(128)}, f32[4,512]{1,0:T(4,128)S(1)}, ...), condition=%wide.region_7.8_spmd.clone, body=%wide.region_2.7_spmd.clone.sunk | while | flops 2149586432 | bytes 10522843 | solution.py:101
  133.7 0.6 dynamic_slice.29
  134.9 5.9 %fusion.105 = (f32[512]{0:T(512)S(1)}, f32[512,512]{0,1:T(8,128)S(1)}) fusion(bf16[4096,512]{1,0:T(8,128)(2,1)} %get-tuple-element.266, bf16[2048,4096]{0,1:T(8,128)(2,1)} %get-tuple-element.265, s32[]{:T(128)S(6)} %select_n.72), kind=kOutput, calls=%fused_computation.187.clone.1 | convolution fusion | flops 2147745280 | bytes 9439236 | tf_op jit(solution)/shard_map/while/body/eval_jaxpr/dot_general | solution.py:85
  140.8 0.8 dynamic_slice.30
  141.6 0.3 multiply_reduce_fusion.2
  142.0 0.1 dynamic_update_slice.22
  142.2 0.6 dynamic_slice.29
  143.4 5.9 %fusion.105 = (f32[512]{0:T(512)S(1)}, f32[512,512]{0,1:T(8,128)S(1)}) fusion(bf16[4096,512]{1,0:T(8,128)(2,1)} %get-tuple-element.266, bf16[2048,4096]{0,1:T(8,128)(2,1)} %get-tuple-element.265, s32[]{:T(128)S(6)} %select_n.72), kind=kOutput, calls=%fused_computation.187.clone.1 | convolution fusion | flops 2147745280 | bytes 9439236 | tf_op jit(solution)/shard_map/while/body/eval_jaxpr/dot_general | solution.py:85
  149.3 0.8 dynamic_slice.30
  150.1 0.3 multiply_reduce_fusion.2
  150.5 0.1 dynamic_update_slice.22
  150.6 0.6 dynamic_slice.29
  151.9 5.9 %fusion.105 = (f32[512]{0:T(512)S(1)}, f32[512,512]{0,1:T(8,128)S(1)}) fusion(bf16[4096,512]{1,0:T(8,128)(2,1)} %get-tuple-element.266, bf16[2048,4096]{0,1:T(8,128)(2,1)} %get-tuple-element.265, s32[]{:T(128)S(6)} %select_n.72), kind=kOutput, calls=%fused_computation.187.clone.1 | convolution fusion | flops 2147745280 | bytes 9439236 | tf_op jit(solution)/shard_map/while/body/eval_jaxpr/dot_general | solution.py:85
  157.7 0.8 dynamic_slice.30
  158.5 0.3 multiply_reduce_fusion.2
  158.9 0.1 dynamic_update_slice.22
  159.1 0.6 dynamic_slice.29
  160.3 5.9 %fusion.105 = (f32[512]{0:T(512)S(1)}, f32[512,512]{0,1:T(8,128)S(1)}) fusion(bf16[4096,512]{1,0:T(8,128)(2,1)} %get-tuple-element.266, bf16[2048,4096]{0,1:T(8,128)(2,1)} %get-tuple-element.265, s32[]{:T(128)S(6)} %select_n.72), kind=kOutput, calls=%fused_computation.187.clone.1 | convolution fusion | flops 2147745280 | bytes 9439236 | tf_op jit(solution)/shard_map/while/body/eval_jaxpr/dot_general | solution.py:85
  166.2 0.8 dynamic_slice.30
  167.0 0.3 multiply_reduce_fusion.2
  167.4 0.1 dynamic_update_slice.22
  167.6 18.8 %all-gather.3 = f32[8,4,2048]{2,1,0:T(4,128)S(1)} all-gather(f32[1,4,2048]{2,1,0:T(4,128)S(1)} %maximum_bitcast_fusion), channel_id=2, replica_groups=mesh['req'=4,'vocab_0'=8,'vocab_1'=4,'vocab_2'=2] {'vocab_0'}, dimensions={0}, use_global_device_ids=true | all-gather | bytes 294912 | tf_op jit(solution)/shard_map/all_gather | solution.py:22
  186.4 0.2 fusion.62
  186.6 0.1 fusion.39
  186.7 0.2 fusion.41
  186.9 9.1 %all-gather.4 = f32[4,4,2048]{2,1,0:T(4,128)S(1)} all-gather(f32[1,4,2048]{2,1,0:T(4,128)S(1)} %maximum_bitcast_fusion.1), channel_id=3, replica_groups=mesh['req'=4,'vocab_0'=8,'vocab_1'=4,'vocab_2'=2] {'vocab_1'}, dimensions={0}, use_global_device_ids=true | all-gather | bytes 163840 | tf_op jit(solution)/shard_map/all_gather | solution.py:22
  196.0 0.1 fusion.31
  196.1 0.1 fusion.22
  196.3 10.7 %all-gather.5 = f32[2,4,2048]{2,1,0:T(4,128)S(1)} all-gather(f32[1,4,2048]{2,1,0:T(4,128)S(1)} %maximum_bitcast_fusion.2), channel_id=4, replica_groups=mesh['req'=4,'vocab_0'=8,'vocab_1'=4,'vocab_2'=2] {'vocab_2'}, dimensions={0}, use_global_device_ids=true | all-gather | bytes 98304 | tf_op jit(solution)/shard_map/all_gather | solution.py:22
  207.0 0.7 subtract_select_fusion
  207.7 0.6 dynamic_slice.17
  208.3 0.6 dynamic_slice.16
  208.9 0.2 select_reduce_fusion.1
  209.1 0.5 fusion.92
  (37 shorter events, 0.9 us)
Async XLA Ops:
  7.2 107.0 %all-gather.8.cloned.1.call-start = ((), (), s32[]{:S(2)}) async-start(), calls=%async_computation.1 | async-start | bytes 17039360 | tf_op jit(solution)/shard_map/all_gather | solution.py:75
  11.6 52.1 %all-to-all-start = ((bf16[4,4096,128]{2,1,0:T(8,128)(2,1)}), bf16[4,4096,128]{2,1,0:T(8,128)(2,1)}, u32[]{:S(2)}, u32[]{:S(2)}) async-start(bf16[4,4096,128]{2,1,0:T(8,128)(2,1)} %stack.2), calls=%async_computation | async-start | bytes 8388608 | tf_op jit(solution)/shard_map/all_to_all | solution.py:80
  18.7 103.2 %copy-start.1 = (f32[4096]{0:T(1024)S(1)}, f32[4096]{0:T(1024)}, u32[]{:S(2)}) copy-start(f32[4096]{0:T(1024)} %param.8) | copy-start | bytes 49156
  114.2 10.8 %copy-start = (bf16[2048,4096]{0,1:T(8,128)(2,1)S(1)}, bf16[2048,4096]{0,1:T(8,128)(2,1)}, u32[]{:S(2)}) copy-start(bf16[2048,4096]{0,1:T(8,128)(2,1)} %all-gather.8.cloned.1.call-done) | copy-start | bytes 50331652
  133.7 75.4 %copy-start.2 = (s32[1,4]{1,0:T(1,128)S(1)}, s32[1,4]{1,0:T(1,128)}, u32[]{:S(2)}) copy-start(s32[1,4]{1,0:T(1,128)} %param.11) | copy-start | bytes 52
Sparse Core Ops, SparseCore 0:
  10.7 103.3 all-gather.7
